TPU v7x, 32 devices: a whole 2x2x4 slice. The times are simulated.
32 devices in a mesh: ctx: 2 (over y), fsdp: 16 (over z, x, core).
Axes of the slice: x: 2, y: 2, z: 4, core: 2. Of those that a mesh axis runs over, the one named last changes fastest.
Arguments:
- tokens: bfloat16 [16, 1024, 768], P('fsdp', 'ctx'), may hold values from -6 to 6
- step_embed: bfloat16 [16, 768], P('fsdp'), may hold values from -3 to 3
- block_ids: int32 [16, 4], P('fsdp', 'ctx'), may hold values from 0 to 3, as said below
- cotangent: bfloat16 [16, 1024, 768], P('fsdp', 'ctx'), may hold values from -6 to 6
- project_weight: float32 [768, 2304], P('fsdp'), may hold values from -0.21875 to 0.21875
- project_bias: float32 [2, 768], P(None, 'fsdp'), may hold values from -2 to 2
- output_weight: float32 [768, 768], P('fsdp'), may hold values from -3 to 3
- output_bias: float32 [768], P('fsdp'), may hold values from -2 to 2
- first_gain: float32 [768], P('fsdp'), may hold values from 0.25 to 1.75
- first_shift: float32 [768], P('fsdp'), may hold values from -2 to 2
- up_weight: float32 [768, 3072], P('fsdp'), may hold values from -0.21875 to 0.21875
- up_bias: float32 [3072], P('fsdp'), may hold values from -3 to 3
- down_weight: float32 [3072, 768], P('fsdp'), may hold values from -0.109375 to 0.109375
- down_bias: float32 [768], P('fsdp'), may hold values from -2 to 2
- second_gain: float32 [768], P('fsdp'), may hold values from 0.25 to 1.75
- second_shift: float32 [768], P('fsdp'), may hold values from -2 to 2
Outputs:
- output: float32 [16, 1024, 768], P('fsdp', 'ctx')
- token_grad: float32 [16, 1024, 768], P('fsdp', 'ctx')
- grad_project_weight: float32 [768, 2304], P('fsdp')
- grad_project_bias: float32 [2, 768], P(None, 'fsdp')
- grad_output_weight: float32 [768, 768], P('fsdp')
- grad_output_bias: float32 [768], P('fsdp')
- grad_first_gain: float32 [768], P('fsdp')
- grad_first_shift: float32 [768], P('fsdp')
- grad_up_weight: float32 [768, 3072], P('fsdp')
- grad_up_bias: float32 [3072], P('fsdp')
- grad_down_weight: float32 [3072, 768], P('fsdp')
- grad_down_bias: float32 [768], P('fsdp')
- grad_second_gain: float32 [768], P('fsdp')
- grad_second_shift: float32 [768], P('fsdp')
Inputs may be any that keep to these rules, and one draw needn't show every extreme that they name: `block_ids`: in every sequence each id appears once, and the two blocks stored on one index of ctx have ids adding to 3.
All inputs are finite; a program needn't handle non-finite values.
Results may differ from a plain program's by a relative error of at most 0.019.
The roundings to bfloat16 on the way count: a program that leaves them out, or rounds other values in their place, can miss the bound.
Values may be sent and summed in bfloat16 or wider, within the bound.
No kernel may reach another device: no remote copies, remote signals or barrier semaphores. Data moves between devices by JAX's collectives and lax.ppermute only.
A program may use at most 192 MiB of HBM per device.

v0:
```python
import jax
import jax.numpy as jnp
from jax import lax
from jax.sharding import PartitionSpec as P

HEADS = 12
norm_epsilon = 1e-05
masked_score = -1e30


def layer_norm(values, gain, shift):
    center = values - jnp.mean(values, axis=-1, keepdims=True)
    spread = jnp.mean(center * center, axis=-1, keepdims=True)
    return center * lax.rsqrt(spread + norm_epsilon) * gain + shift


def gelu_exact(values):
    return jax.nn.gelu(values, approximate=False)


def product(left, right):
    return jnp.dot(left, right, preferred_element_type=jnp.float32)


def transpose_left(left, right):
    return lax.dot_general(
        left, right, (((0,), (0,)), ((), ())), preferred_element_type=jnp.float32
    )


def transpose_right(left, right):
    return lax.dot_general(
        left, right, (((1,), (1,)), ((), ())), preferred_element_type=jnp.float32
    )


def column_sum(values):
    return jnp.sum(values.astype(jnp.float32), axis=0)


def shards(
    tokens,
    step_embed,
    block_ids,
    cotangent,
    project_weight,
    project_bias,
    output_weight,
    output_bias,
    first_gain,
    first_shift,
    up_weight,
    up_bias,
    down_weight,
    down_bias,
    second_gain,
    second_shift,
):
    gathered = (
        lax.all_gather(project_weight.astype(jnp.bfloat16), "fsdp", axis=0, tiled=True),
        lax.all_gather(project_bias.astype(jnp.bfloat16), "fsdp", axis=1, tiled=True),
        lax.all_gather(output_weight.astype(jnp.bfloat16), "fsdp", axis=0, tiled=True),
        lax.all_gather(output_bias.astype(jnp.bfloat16), "fsdp", axis=0, tiled=True),
        lax.all_gather(first_gain.astype(jnp.bfloat16), "fsdp", axis=0, tiled=True),
        lax.all_gather(first_shift.astype(jnp.bfloat16), "fsdp", axis=0, tiled=True),
        lax.all_gather(up_weight.astype(jnp.bfloat16), "fsdp", axis=0, tiled=True),
        lax.all_gather(up_bias.astype(jnp.bfloat16), "fsdp", axis=0, tiled=True),
        lax.all_gather(down_weight.astype(jnp.bfloat16), "fsdp", axis=0, tiled=True),
        lax.all_gather(down_bias.astype(jnp.bfloat16), "fsdp", axis=0, tiled=True),
        lax.all_gather(second_gain.astype(jnp.bfloat16), "fsdp", axis=0, tiled=True),
        lax.all_gather(second_shift.astype(jnp.bfloat16), "fsdp", axis=0, tiled=True),
    )
    (
        project_matrix,
        project_offset,
        output_matrix,
        output_offset,
        first_scale,
        first_offset,
        up_matrix,
        up_offset,
        down_matrix,
        down_offset,
        second_scale,
        second_offset,
    ) = gathered
    seq_count, pair_rows, width = tokens.shape
    head_dim = width // HEADS
    pair_width = 2 * head_dim
    pair_count = HEADS // 2
    scale = head_dim ** (-0.5)
    flat_rows = seq_count * pair_rows
    pair_indices = jnp.arange(pair_count, dtype=jnp.int32)

    def head_pair(source, pair_index):
        piece = lax.dynamic_slice_in_dim(source, pair_index * pair_width, pair_width, 2)
        return piece.reshape(seq_count, source.shape[1], 2, head_dim)

    def merge_pairs(stacked):
        return jnp.transpose(stacked, (1, 2, 0, 3)).reshape(flat_rows, width)

    hidden_zero = (tokens.astype(jnp.float32) + step_embed.astype(jnp.float32)[:, None, :]).reshape(
        flat_rows, width
    )
    hidden_zero_low = hidden_zero.astype(jnp.bfloat16)
    offsets = project_offset.astype(jnp.float32)
    bias_row = jnp.concatenate([offsets[0], jnp.zeros_like(offsets[0]), offsets[1]])
    projected = (product(hidden_zero_low, project_matrix) + bias_row).astype(jnp.bfloat16)
    queries = projected[:, :width].reshape(seq_count, pair_rows, width)
    keys_here = projected[:, width : 2 * width].reshape(seq_count, pair_rows, width)
    values_here = projected[:, 2 * width :].reshape(seq_count, pair_rows, width)
    keys_all, values_all, ids_all = (
        lax.all_gather(keys_here, "ctx", axis=1, tiled=True),
        lax.all_gather(values_here, "ctx", axis=1, tiled=True),
        lax.all_gather(block_ids.astype(jnp.bfloat16), "ctx", axis=1, tiled=True),
    )
    block_rows = pair_rows // block_ids.shape[1]
    query_ids = jnp.repeat(block_ids, block_rows, axis=1)
    key_ids = jnp.repeat(ids_all.astype(jnp.int32), block_rows, axis=1)
    allowed = key_ids[:, None, None, :] <= query_ids[:, None, :, None]

    def forward_pair(pair_index):
        query_pair = head_pair(queries, pair_index)
        key_pair = head_pair(keys_all, pair_index)
        value_pair = head_pair(values_all, pair_index)
        scores = (
            jnp.einsum("bqhd,bkhd->bhqk", query_pair, key_pair, preferred_element_type=jnp.float32)
            * scale
        )
        scores = jnp.where(allowed, scores, masked_score)
        peak = jnp.max(scores, axis=-1, keepdims=True)
        expon = jnp.exp(scores - peak)
        totals = jnp.sum(expon, axis=-1, keepdims=True)
        probs = expon / totals
        mixed_pair = jnp.einsum(
            "bhqk,bkhd->bqhd",
            probs.astype(jnp.bfloat16),
            value_pair,
            preferred_element_type=jnp.float32,
        )
        log_total = (peak + jnp.log(totals))[..., 0]
        return (
            mixed_pair.astype(jnp.bfloat16).reshape(seq_count, pair_rows, pair_width),
            log_total,
        )

    mixed_pairs, log_totals = lax.map(forward_pair, pair_indices)
    mixed = merge_pairs(mixed_pairs)
    branch = product(mixed, output_matrix) + output_offset.astype(jnp.float32)
    hidden_one, first_pull = jax.vjp(
        layer_norm,
        hidden_zero + branch,
        first_scale.astype(jnp.float32),
        first_offset.astype(jnp.float32),
    )
    hidden_one_low = hidden_one.astype(jnp.bfloat16)
    inner = product(hidden_one_low, up_matrix) + up_offset.astype(jnp.float32)
    activated, gelu_pull = jax.vjp(gelu_exact, inner)
    activated_low = activated.astype(jnp.bfloat16)
    feed = product(activated_low, down_matrix) + down_offset.astype(jnp.float32)
    result, second_pull = jax.vjp(
        layer_norm,
        hidden_one + feed,
        second_scale.astype(jnp.float32),
        second_offset.astype(jnp.float32),
    )
    project_back, output_back, up_back, down_back = (
        lax.all_gather(project_weight.astype(jnp.bfloat16), "fsdp", axis=0, tiled=True),
        lax.all_gather(output_weight.astype(jnp.bfloat16), "fsdp", axis=0, tiled=True),
        lax.all_gather(up_weight.astype(jnp.bfloat16), "fsdp", axis=0, tiled=True),
        lax.all_gather(down_weight.astype(jnp.bfloat16), "fsdp", axis=0, tiled=True),
    )
    grad_second_in, grad_second_gain, grad_second_shift = second_pull(
        cotangent.reshape(flat_rows, width).astype(jnp.float32)
    )
    feed_grad = grad_second_in.astype(jnp.bfloat16)
    grad_down_bias = column_sum(feed_grad)
    grad_down_weight = transpose_left(activated_low, feed_grad)
    activated_grad = transpose_right(feed_grad, down_back)
    inner_grad = gelu_pull(activated_grad)[0].astype(jnp.bfloat16)
    grad_up_bias = column_sum(inner_grad)
    grad_up_weight = transpose_left(hidden_one_low, inner_grad)
    hidden_one_grad = grad_second_in + transpose_right(inner_grad, up_back)
    grad_first_in, grad_first_gain, grad_first_shift = first_pull(hidden_one_grad)
    branch_grad = grad_first_in.astype(jnp.bfloat16)
    grad_output_bias = column_sum(branch_grad)
    grad_output_weight = transpose_left(mixed, branch_grad)
    mixed_grad = (
        transpose_right(branch_grad, output_back)
        .astype(jnp.bfloat16)
        .reshape(seq_count, pair_rows, width)
    )

    def backward_pair(pair_inputs):
        pair_index, log_total = pair_inputs
        query_pair = head_pair(queries, pair_index)
        key_pair = head_pair(keys_all, pair_index)
        value_pair = head_pair(values_all, pair_index)
        grad_pair = head_pair(mixed_grad, pair_index)
        scores = (
            jnp.einsum("bqhd,bkhd->bhqk", query_pair, key_pair, preferred_element_type=jnp.float32)
            * scale
        )
        probs = jnp.where(allowed, jnp.exp(scores - log_total[..., None]), 0.0)
        prob_grad = jnp.einsum(
            "bqhd,bkhd->bhqk", grad_pair, value_pair, preferred_element_type=jnp.float32
        )
        row_dot = jnp.sum(probs * prob_grad, axis=-1, keepdims=True)
        score_grad = (probs * (prob_grad - row_dot)).astype(jnp.bfloat16)
        query_grad = (
            jnp.einsum("bhqk,bkhd->bqhd", score_grad, key_pair, preferred_element_type=jnp.float32)
            * scale
        )
        key_grad = (
            jnp.einsum(
                "bhqk,bqhd->bkhd", score_grad, query_pair, preferred_element_type=jnp.float32
            )
            * scale
        )
        value_grad = jnp.einsum(
            "bhqk,bqhd->bkhd",
            probs.astype(jnp.bfloat16),
            grad_pair,
            preferred_element_type=jnp.float32,
        )
        return (
            query_grad.astype(jnp.bfloat16).reshape(seq_count, pair_rows, pair_width),
            key_grad.reshape(seq_count, key_pair.shape[1], pair_width),
            value_grad.reshape(seq_count, key_pair.shape[1], pair_width),
        )

    query_grads, key_partial, value_partial = lax.map(backward_pair, (pair_indices, log_totals))
    key_sums, value_sums = (
        lax.psum_scatter(
            key_partial.astype(jnp.bfloat16), "ctx", scatter_dimension=2, tiled=True
        ).astype(jnp.float32),
        lax.psum_scatter(
            value_partial.astype(jnp.bfloat16), "ctx", scatter_dimension=2, tiled=True
        ).astype(jnp.float32),
    )
    key_grads = key_sums.astype(jnp.bfloat16)
    value_grads = value_sums.astype(jnp.bfloat16)
    project_grad = jnp.concatenate(
        [merge_pairs(query_grads), merge_pairs(key_grads), merge_pairs(value_grads)], axis=1
    )
    grad_project_bias = jnp.stack(
        [column_sum(project_grad[:, :width]), column_sum(project_grad[:, 2 * width :])]
    )
    grad_project_weight = transpose_left(hidden_zero_low, project_grad)
    input_grad = grad_first_in + transpose_right(project_grad, project_back)
    shares = (
        lax.psum_scatter(
            grad_project_weight.astype(jnp.bfloat16), "fsdp", scatter_dimension=0, tiled=True
        ).astype(jnp.float32),
        lax.psum_scatter(
            grad_project_bias.astype(jnp.bfloat16), "fsdp", scatter_dimension=1, tiled=True
        ).astype(jnp.float32),
        lax.psum_scatter(
            grad_output_weight.astype(jnp.bfloat16), "fsdp", scatter_dimension=0, tiled=True
        ).astype(jnp.float32),
        lax.psum_scatter(
            grad_output_bias.astype(jnp.bfloat16), "fsdp", scatter_dimension=0, tiled=True
        ).astype(jnp.float32),
        lax.psum_scatter(
            grad_first_gain.astype(jnp.bfloat16), "fsdp", scatter_dimension=0, tiled=True
        ).astype(jnp.float32),
        lax.psum_scatter(
            grad_first_shift.astype(jnp.bfloat16), "fsdp", scatter_dimension=0, tiled=True
        ).astype(jnp.float32),
        lax.psum_scatter(
            grad_up_weight.astype(jnp.bfloat16), "fsdp", scatter_dimension=0, tiled=True
        ).astype(jnp.float32),
        lax.psum_scatter(
            grad_up_bias.astype(jnp.bfloat16), "fsdp", scatter_dimension=0, tiled=True
        ).astype(jnp.float32),
        lax.psum_scatter(
            grad_down_weight.astype(jnp.bfloat16), "fsdp", scatter_dimension=0, tiled=True
        ).astype(jnp.float32),
        lax.psum_scatter(
            grad_down_bias.astype(jnp.bfloat16), "fsdp", scatter_dimension=0, tiled=True
        ).astype(jnp.float32),
        lax.psum_scatter(
            grad_second_gain.astype(jnp.bfloat16), "fsdp", scatter_dimension=0, tiled=True
        ).astype(jnp.float32),
        lax.psum_scatter(
            grad_second_shift.astype(jnp.bfloat16), "fsdp", scatter_dimension=0, tiled=True
        ).astype(jnp.float32),
    )
    summed = (
        lax.psum(shares[0].astype(jnp.bfloat16), "ctx").astype(jnp.float32),
        lax.psum(shares[1].astype(jnp.bfloat16), "ctx").astype(jnp.float32),
        lax.psum(shares[2].astype(jnp.bfloat16), "ctx").astype(jnp.float32),
        lax.psum(shares[3].astype(jnp.bfloat16), "ctx").astype(jnp.float32),
        lax.psum(shares[4].astype(jnp.bfloat16), "ctx").astype(jnp.float32),
        lax.psum(shares[5].astype(jnp.bfloat16), "ctx").astype(jnp.float32),
        lax.psum(shares[6].astype(jnp.bfloat16), "ctx").astype(jnp.float32),
        lax.psum(shares[7].astype(jnp.bfloat16), "ctx").astype(jnp.float32),
        lax.psum(shares[8].astype(jnp.bfloat16), "ctx").astype(jnp.float32),
        lax.psum(shares[9].astype(jnp.bfloat16), "ctx").astype(jnp.float32),
        lax.psum(shares[10].astype(jnp.bfloat16), "ctx").astype(jnp.float32),
        lax.psum(shares[11].astype(jnp.bfloat16), "ctx").astype(jnp.float32),
    )
    return (
        result.reshape(seq_count, pair_rows, width),
        input_grad.reshape(seq_count, pair_rows, width),
        summed[0],
        summed[1],
        summed[2],
        summed[3],
        summed[4],
        summed[5],
        summed[6],
        summed[7],
        summed[8],
        summed[9],
        summed[10],
        summed[11],
    )


def solution(mesh):
    return jax.shard_map(
        shards,
        mesh=mesh,
        in_specs=(
            P("fsdp", "ctx", None),
            P("fsdp", None),
            P("fsdp", "ctx"),
            P("fsdp", "ctx", None),
            P("fsdp", None),
            P(None, "fsdp"),
            P("fsdp", None),
            P("fsdp"),
            P("fsdp"),
            P("fsdp"),
            P("fsdp", None),
            P("fsdp"),
            P("fsdp", None),
            P("fsdp"),
            P("fsdp"),
            P("fsdp"),
        ),
        out_specs=(
            P("fsdp", "ctx", None),
            P("fsdp", "ctx", None),
            P("fsdp", None),
            P(None, "fsdp"),
            P("fsdp", None),
            P("fsdp"),
            P("fsdp"),
            P("fsdp"),
            P("fsdp", None),
            P("fsdp"),
            P("fsdp", None),
            P("fsdp"),
            P("fsdp"),
            P("fsdp"),
        ),
        check_vma=False,
    )
```

profile of v0, /device:TPU:0, one launch (start us, length us, event | category | flops | bytes accessed | tf_op | source)
XLA Modules:
  0.0 857.9 jit_solution(12785414366772415956)
XLA Ops:
  9.7 23.0 %all-gather.2 = bf16[16,48,2]{1,2,0:T(2,128)(2,1)S(1)} all-gather(bf16[1,48,2]{1,2,0:T(2,128)(2,1)S(1)} %convert_bitcast_fusion.1), channel_id=1, replica_groups=mesh['ctx'=2,'fsdp'=16] {'fsdp'}, dimensions={0}, use_global_device_ids=true | all-gather | bytes 3264 | tf_op jit(solution)/shard_map/all_gather | solution.py:61
  33.5 27.3 %all-gather.10.cloned.1.call-done = bf16[768,2304]{1,0:T(8,128)(2,1)} async-done(((bf16[48,2304]{1,0:T(8,128)(2,1)}), bf16[768,2304]{1,0:T(8,128)(2,1)}) %all-gather.10.cloned.1.call-update) | async-done | bytes 3538960 | tf_op jit(solution)/shard_map/all_gather | solution.py:60
  74.6 59.6 %all-reduce.16 = (bf16[768]{0:T(1024)(128)(2,1)S(1)}, bf16[768]{0:T(1024)(128)(2,1)S(1)}, bf16[768]{0:T(1024)(128)(2,1)S(1)}, bf16[3072]{0:T(1024)(128)(2,1)S(1)...) all-reduce(bf16[768]{0:T(1024)(128)(2,1)S(1)} %dynamic-update-slice, ...), channel_id=1, replica_groups=mesh['ctx'=2,'fsdp'=16] {'fsdp'}, use_global_device_ids=true, to_apply=%add.1 | all-reduce | flops 6912 | bytes 27648
  134.2 5.2 all-reduce
  145.3 41.9 %while.28 = (s32[]{:T(128)}, bf16[6,1,512,128]{2,3,1,0:T(8,128)(2,1)}, f32[6,1,2,512]{3,2,1,0:T(2,128)S(1)}, s32[6]{0:T(128)S(1)}, bf16[1,1024,768]{1,2,0:T(8,12...) while((s32[]{:T(128)}, ...), condition=%wide.region_3.4_spmd.clone, body=%wide.region_0.3_spmd.clone.sunk | while | flops 281607168 | bytes 17078980 | solution.py:147
  191.9 26.7 %all-gather.14.cloned.1.call-done = bf16[768,3072]{1,0:T(8,128)(2,1)} async-done(((bf16[48,3072]{1,0:T(8,128)(2,1)}), bf16[768,3072]{1,0:T(8,128)(2,1)}) %all-gather.14.cloned.1.call-update) | async-done | bytes 4718608 | tf_op jit(solution)/shard_map/all_gather | solution.py:66
  218.6 21.3 %multiply_convert_fusion.1 = (bf16[512,3072]{1,0:T(8,128)(2,1)}, f32[512,3072]{1,0:T(8,128)}, f32[512,3072]{1,0:T(8,128)}) fusion(f32[3072]{0:T(1024)S(1)} %convert_element_type.262, bf16[768,3072]{1,0:T(8,128)(2,1)} %all-gather.14.cloned.1.call-done, f32[512,768]{1,0:T(8,128)} %copy-done.8, f32[768]{0:T(1024)S(1)} %convert_element_type.258, ...), kind=kOutput, calls=%fused_computation.40 | convolution fusion | flops 2521694208 | bytes 22042624 | tf_op jit(solution)/shard_map/dot_general | solution.py:22
  240.0 33.4 %all-gather.16.cloned.1.call-done = bf16[3072,768]{1,0:T(8,128)(2,1)} async-done(((bf16[192,768]{1,0:T(8,128)(2,1)}), bf16[3072,768]{1,0:T(8,128)(2,1)}) %all-gather.16.cloned.1.call-update) | async-done | bytes 4718608 | tf_op jit(solution)/shard_map/all_gather | solution.py:68
  273.3 6.5 fusion.46
  283.6 9.2 %fusion.38 = (bf16[3072]{0:T(1024)(128)(2,1)S(1)}, bf16[512,3072]{1,0:T(8,128)(2,1)}) fusion(f32[512,3072]{1,0:T(8,128)} %get-tuple-element.341, f32[512,3072]{1,0:T(8,128)} %get-tuple-element.357, f32[3072]{0:T(1024)S(1)} %convert_element_type.262, bf16[512,768]{1,0:T(8,128)(2,1)S(1)} %get-tuple-element.331, bf16[3072,768]{1,0:T(8,128)(2,1)S(1)} %copy-done.20), kind=kOutput, calls=%fused_computation.115 | convolution fusion | flops 2441081856 | bytes 21252096 | tf_op jit(solution)/shard_map/dot_general | solution.py:32
  292.8 5.1 multiply_reduce_fusion.1
  303.6 101.8 %while.29 = (s32[]{:T(128)}, bf16[6,1,512,128]{2,3,1,0:T(8,128)(2,1)}, bf16[6,1,1024,128]{2,3,1,0:T(8,128)(2,1)}, bf16[6,1,1024,128]{2,3,1,0:T(8,128)(2,1)}, s32...) while((s32[]{:T(128)}, ...), condition=%wide.region_14.15_spmd.clone, body=%wide.region_12.14_spmd.clone.sunk | while | flops 687733760 | bytes 68062520 | solution.py:232
  409.5 7.0 convolution_convert_fusion
  417.9 6.5 convolution_convert_fusion.1
  424.7 5.5 reduce-scatter.12.cloned.1.call-done
  430.2 29.0 %reduce-scatter.10.cloned.1.call-done = bf16[6,1,512,128]{2,3,1,0:T(8,128)(2,1)} async-done(((bf16[6,1,1024,128]{2,3,1,0:T(8,128)(2,1)}), bf16[6,1,512,128]{2,3,1,0:T(8,128)(2,1)}) %reduce-scatter.10.cloned.1.call-update) | async-done | bytes 786448 | tf_op jit(solution)/shard_map/reduce_scatter | solution.py:234
  459.2 5.4 convolution_convert_fusion.2
  469.2 61.3 %all-reduce.15 = (bf16[768]{0:T(1024)(128)(2,1)S(1)}, bf16[768]{0:T(1024)(128)(2,1)S(1)}, bf16[768]{0:T(1024)(128)(2,1)S(1)}, bf16[768]{0:T(1024)(128)(2,1)S(1)}...) all-reduce(bf16[768]{0:T(1024)(128)(2,1)S(1)} %dynamic-update-slice, ...), channel_id=1, replica_groups=mesh['ctx'=2,'fsdp'=16] {'fsdp'}, use_global_device_ids=true, to_apply=%add.7 | all-reduce | flops 8448 | bytes 33792
  531.0 68.3 %reduce-scatter.20.cloned.1.call-done = bf16[192,768]{1,0:T(8,128)(2,1)} async-done(((bf16[3072,768]{1,0:T(8,128)(2,1)}), bf16[192,768]{1,0:T(8,128)(2,1)}) %reduce-scatter.20.cloned.1.call-update) | async-done | bytes 294928 | tf_op jit(solution)/shard_map/reduce_scatter | solution.py:276
  599.3 79.1 %reduce-scatter.18.cloned.1.call-done = bf16[48,3072]{1,0:T(8,128)(2,1)} async-done(((bf16[768,3072]{1,0:T(8,128)(2,1)}), bf16[48,3072]{1,0:T(8,128)(2,1)}) %reduce-scatter.18.cloned.1.call-update) | async-done | bytes 294928 | tf_op jit(solution)/shard_map/reduce_scatter | solution.py:270
  678.4 70.8 %reduce-scatter.14.cloned.1.call-done = bf16[48,2304]{1,0:T(8,128)(2,1)} async-done(((bf16[768,2304]{1,0:T(8,128)(2,1)}), bf16[48,2304]{1,0:T(8,128)(2,1)}) %reduce-scatter.14.cloned.1.call-update) | async-done | bytes 221200 | tf_op jit(solution)/shard_map/reduce_scatter | solution.py:252
  750.7 5.9 add_bitcast_fusion
  756.6 49.2 %reduce-scatter.22.cloned.1.call-done = bf16[48,2]{1,0:T(8,128)(2,1)} async-done(((bf16[768,2]{1,0:T(8,128)(2,1)}), bf16[48,2]{1,0:T(8,128)(2,1)}) %reduce-scatter.22.cloned.1.call-update) | async-done | bytes 208
  815.7 28.5 %all-reduce.21.cloned.1.call-done = (bf16[48,2304]{1,0:T(8,128)(2,1)}, bf16[48,768]{1,0:T(8,128)(2,1)}, bf16[48,3072]{1,0:T(8,128)(2,1)}, bf16[192,768]{1,0:T(8,128)(2,1)}) async-done(((bf16[48,2304]{1,0:T(8,128)(2,1)}, bf16[48,768]{1,0:T(8,128)(2,1)}, bf16[48,3072]{1,0:T(8,128)(2,1)}, bf16[192,768]{1,0:T(8,128)(2,1)}), (bf16[48,2304]{1,0:T(8,128)(2,1)}, bf16[48,768]{1,0:T(8,128)(2,1)}, ...) | async-done | bytes 884752 | tf_op jit(solution)/shard_map/psum | solution.py:290
  (386 shorter events, 197.1 us)
Async XLA Ops:
  7.2 53.6 %all-gather.10.cloned.1.call-start = ((), (), s32[]{:S(2)}) async-start(), calls=%async_computation.7 | async-start | bytes 3760128 | tf_op jit(solution)/shard_map/all_gather | solution.py:60
  9.0 131.9 %all-gather.18.cloned.1.call-start = ((), (), s32[]{:S(2)}) async-start(), calls=%async_computation.17 | async-start | bytes 2359296 | tf_op jit(solution)/shard_map/all_gather | solution.py:114
  65.2 6.6 copy-start.23
  65.2 6.6 copy-start.30
  65.2 7.2 copy-start.19
  66.5 76.0 %all-gather.20.cloned.1.call-start = ((), (), s32[]{:S(2)}) async-start(), calls=%async_computation.18 | async-start | bytes 2359296 | tf_op jit(solution)/shard_map/all_gather | solution.py:113
  67.3 120.0 %all-gather.12.cloned.1.call-start = ((), (), s32[]{:S(2)}) async-start(), calls=%async_computation.8 | async-start | bytes 1253376 | tf_op jit(solution)/shard_map/all_gather | solution.py:62
  68.0 150.6 %all-gather.14.cloned.1.call-start = ((), (), s32[]{:S(2)}) async-start(), calls=%async_computation.9 | async-start | bytes 5013504 | tf_op jit(solution)/shard_map/all_gather | solution.py:66
  68.8 204.5 %all-gather.16.cloned.1.call-start = ((), (), s32[]{:S(2)}) async-start(), calls=%async_computation.10 | async-start | bytes 5013504 | tf_op jit(solution)/shard_map/all_gather | solution.py:68
  69.7 360.5 %reduce-scatter.12.cloned.1.call-start = ((), (), s32[]{:S(2)}) async-start(), calls=%async_computation.12 | async-start | bytes 2359296 | tf_op jit(solution)/shard_map/reduce_scatter | solution.py:237
  273.3 6.9 copy-start.4
  281.6 11.1 %slice-start = ((s8[4718592]{0:T(1024)(128)(4,1)}), s8[4194304]{0:T(1024)(128)(4,1)S(1)}, s32[]{:S(2)}) async-start(s8[4718592]{0:T(1024)(128)(4,1)} %bitcast.216), calls=%async_computation.21 | async-start | bytes 8388608
  281.9 10.9 %copy-start.12 = (bf16[512,768]{1,0:T(8,128)(2,1)}, bf16[512,768]{1,0:T(8,128)(2,1)S(1)}, u32[]{:S(2)}) copy-start(bf16[512,768]{1,0:T(8,128)(2,1)S(1)} %get-tuple-element.331) | copy-start | bytes 2359300
  283.6 9.2 %copy-start.9 = (f32[512,768]{1,0:T(8,128)S(1)}, f32[512,768]{1,0:T(8,128)}, u32[]{:S(2)}) copy-start(f32[512,768]{1,0:T(8,128)} %copy-done.8) | copy-start | bytes 4718596
  283.6 9.2 %slice-start.1 = ((s8[4718592]{0:T(1024)(128)(4,1)}), s8[524288]{0:T(1024)(128)(4,1)S(1)}, s32[]{:S(2)}) async-start(s8[4718592]{0:T(1024)(128)(4,1)} %bitcast.216), calls=%async_computation.22 | async-start | bytes 1048576
  405.4 53.8 %reduce-scatter.10.cloned.1.call-start = ((), (), s32[]{:S(2)}) async-start(), calls=%async_computation.11 | async-start | bytes 2359296 | tf_op jit(solution)/shard_map/reduce_scatter | solution.py:234
  406.2 124.8 %reduce-scatter.16.cloned.1.call-start = ((), (), s32[]{:S(2)}) async-start(), calls=%async_computation.14 | async-start | bytes 1253376 | tf_op jit(solution)/shard_map/reduce_scatter | solution.py:258
  409.4 189.9 %reduce-scatter.20.cloned.1.call-start = ((), (), s32[]{:S(2)}) async-start(), calls=%async_computation.16 | async-start | bytes 5013504 | tf_op jit(solution)/shard_map/reduce_scatter | solution.py:276
  416.5 261.8 %reduce-scatter.18.cloned.1.call-start = ((), (), s32[]{:S(2)}) async-start(), calls=%async_computation.15 | async-start | bytes 5013504 | tf_op jit(solution)/shard_map/reduce_scatter | solution.py:270
  424.4 34.8 %copy-start.22 = (bf16[1,512,768]{2,1,0:T(8,128)(2,1)S(1)}, bf16[1,512,768]{2,1,0:T(8,128)(2,1)}, u32[]{:S(2)}) copy-start(bf16[1,512,768]{2,1,0:T(8,128)(2,1)} %param.20) | copy-start | bytes 2359300
  424.5 324.8 %reduce-scatter.14.cloned.1.call-start = ((), (), s32[]{:S(2)}) async-start(), calls=%async_computation.13 | async-start | bytes 3760128 | tf_op jit(solution)/shard_map/reduce_scatter | solution.py:252
  464.7 341.1 %reduce-scatter.22.cloned.1.call-start = ((), (), s32[]{:S(2)}) async-start(), calls=%async_computation.19 | async-start | bytes 208896
  467.3 377.0 %all-reduce.21.cloned.1.call-start = ((), (), s32[]{:S(2)}) async-start(), calls=%async_computation.20 | async-start | bytes 1769472 | tf_op jit(solution)/shard_map/psum | solution.py:290
  467.5 283.2 %copy-start.7 = (f32[512,768]{1,0:T(8,128)S(1)}, f32[512,768]{1,0:T(8,128)}, u32[]{:S(2)}) copy-start(f32[512,768]{1,0:T(8,128)} %copy-done.6) | copy-start | bytes 4718596
  (38 other events, 109.6 us)
Sparse Core Ops, SparseCore 0:
  10.9 49.8 all-gather.9
  66.7 26.2 all-gather.17
  95.0 27.2 all-gather.19
  125.0 38.3 all-gather.11
  166.2 52.4 all-gather.13
  221.4 51.9 all-gather.15
  405.5 24.6 reduce-scatter.11
  433.1 26.0 reduce-scatter.9
  462.8 58.0 reduce-scatter.15
  524.7 74.5 reduce-scatter.19
  603.6 74.6 reduce-scatter.17
  682.1 67.0 reduce-scatter.13
  753.3 52.4 reduce-scatter.21
  808.2 36.0 all-reduce.20
where the time goes:
time: 864 us; the launch traced here: 858 us
  waiting for transfers between devices  419 us (48%)
  blocking collectives  154 us (18%)
  matrix products  151 us (17%)
  local copies, waits for them, and re-layouts  63.7 us (7%)
  other arithmetic  42.3 us (5%)
  between operations  18.2 us (2%)
  loops' own time  8.76 us (1%)
    unnamed x3, blocking collectives  126 us
    reduce_scatter x1, waiting for transfers between devices, shards(): lax.psum_scatter(grad_up_weight.astype(jnp.bfloat16), 'fsdp', scatter_dim...  79.1 us
    reduce_scatter x1, waiting for transfers between devices, shards(): lax.psum_scatter(grad_project_weight.astype(jnp.bfloat16), 'fsdp', scatte...  70.8 us
    reduce_scatter x1, waiting for transfers between devices, shards(): lax.psum_scatter(grad_down_weight.astype(jnp.bfloat16), 'fsdp', scatter_d...  68.3 us
    unnamed x15, waiting for transfers between devices  50.8 us
    dot_general x4, matrix products, product(): return jnp.dot(left, right, preferred_element_type=jnp.float32)  35.3 us
    all_gather x1, waiting for transfers between devices, shards(): lax.all_gather(down_weight.astype(jnp.bfloat16), 'fsdp', axis=0, tiled=True)  33.4 us
    reduce_scatter x1, waiting for transfers between devices, shards(): lax.psum_scatter(key_partial.astype(jnp.bfloat16), 'ctx', scatter_dimensi...  29 us
  transfers between devices with their start and end apart: 14, of which 10 were waited for; matrix products, arithmetic and copies ran while one was open for 13% of the time, Pallas kernels for 0%

commit v1 on v0

--- a/solution.py
+++ b/solution.py
@@ -287,7 +287,7 @@
         ).astype(jnp.float32),
     )
     summed = (
-        lax.psum(shares[0].astype(jnp.bfloat16), "ctx").astype(jnp.float32),
+        jnp.sum(lax.all_gather(shares[0].astype(jnp.bfloat16), "ctx"), axis=0).astype(jnp.float32),
         lax.psum(shares[1].astype(jnp.bfloat16), "ctx").astype(jnp.float32),
         lax.psum(shares[2].astype(jnp.bfloat16), "ctx").astype(jnp.float32),
         lax.psum(shares[3].astype(jnp.bfloat16), "ctx").astype(jnp.float32),

time: 864 us -> 873 us (1.010)
  waiting for transfers between devices: 419 us -> 400 us
  local copies, waits for them, and re-layouts: 63.7 us -> 77.8 us
    reduce_scatter x1, waiting for transfers between devices: 0.01 us -> 60.3 us  [shards(): lax.psum_scatter(grad_output_weight.astype(jnp.bfloat16), 'fsdp', scatter...]
    unnamed x15, waiting for transfers between devices: 50.8 us -> 1.56 us
    psum x1, waiting for transfers between devices: 28.5 us -> 3.52 us  [shards(): lax.psum(shares[2].astype(jnp.bfloat16), 'ctx').astype(jnp.float32)]
    all_gather x1, waiting for transfers between devices: 26.7 us -> 16 us  [shards(): lax.all_gather(up_weight.astype(jnp.bfloat16), 'fsdp', axis=0, tiled=True)]
    reduce_scatter x1, waiting for transfers between devices: 68.3 us -> 78.3 us  [shards(): lax.psum_scatter(grad_down_weight.astype(jnp.bfloat16), 'fsdp', scatter_d...]
  transfers between devices with their start and end apart: 14 -> 14, of which waited for: 10 -> 10; matrix products, arithmetic and copies ran while one was open for 13% -> 15% of each run, Pallas kernels for 0% -> 0%
where the time goes in v1:
time: 873 us; the launch traced here: 866 us
  waiting for transfers between devices  400 us (46%)
  blocking collectives  161 us (18%)
  matrix products  151 us (17%)
  local copies, waits for them, and re-layouts  77.8 us (9%)
  other arithmetic  48.7 us (6%)
  between operations  18.1 us (2%)
    unnamed x3, blocking collectives  126 us
    reduce_scatter x1, waiting for transfers between devices, shards(): lax.psum_scatter(grad_up_weight.astype(jnp.bfloat16), 'fsdp', scatter_dim...  79 us
    reduce_scatter x1, waiting for transfers between devices, shards(): lax.psum_scatter(grad_down_weight.astype(jnp.bfloat16), 'fsdp', scatter_d...  78.3 us
    reduce_scatter x1, waiting for transfers between devices, shards(): lax.psum_scatter(grad_project_weight.astype(jnp.bfloat16), 'fsdp', scatte...  67.3 us
    reduce_scatter x1, waiting for transfers between devices, shards(): lax.psum_scatter(grad_output_weight.astype(jnp.bfloat16), 'fsdp', scatter...  60.3 us
    all_gather x1, waiting for transfers between devices, shards(): lax.all_gather(down_weight.astype(jnp.bfloat16), 'fsdp', axis=0, tiled=True)  34.4 us
    dot_general x4, matrix products, product(): return jnp.dot(left, right, preferred_element_type=jnp.float32)  33.6 us
    dynamic_slice x42, local copies, waits for them, and re-layouts, head_pair(): lax.dynamic_slice_in_dim(source, pair_index * pair_width, pair_width, 2)  29.2 us
  transfers between devices with their start and end apart: 14, of which 10 were waited for; matrix products, arithmetic and copies ran while one was open for 15% of the time, Pallas kernels for 0%

profile of v1, /device:TPU:0, one launch (start us, length us, event | category | flops | bytes accessed | tf_op | source)
XLA Modules:
  0.0 866.2 jit_solution(2566838862846077224)
XLA Ops:
  9.7 23.0 %all-gather.3 = bf16[16,48,2]{1,2,0:T(2,128)(2,1)S(1)} all-gather(bf16[1,48,2]{1,2,0:T(2,128)(2,1)S(1)} %convert_bitcast_fusion.1), channel_id=1, replica_groups=mesh['ctx'=2,'fsdp'=16] {'fsdp'}, dimensions={0}, use_global_device_ids=true | all-gather | bytes 3264 | tf_op jit(solution)/shard_map/all_gather | solution.py:61
  33.5 27.2 %all-gather.11.cloned.1.call-done = bf16[768,2304]{1,0:T(8,128)(2,1)} async-done(((bf16[48,2304]{1,0:T(8,128)(2,1)}), bf16[768,2304]{1,0:T(8,128)(2,1)}) %all-gather.11.cloned.1.call-update) | async-done | bytes 3538960 | tf_op jit(solution)/shard_map/all_gather | solution.py:60
  75.1 59.7 %all-reduce.16 = (bf16[768]{0:T(1024)(128)(2,1)S(1)}, bf16[768]{0:T(1024)(128)(2,1)S(1)}, bf16[768]{0:T(1024)(128)(2,1)S(1)}, bf16[3072]{0:T(1024)(128)(2,1)S(1)...) all-reduce(bf16[768]{0:T(1024)(128)(2,1)S(1)} %dynamic-update-slice, ...), channel_id=1, replica_groups=mesh['ctx'=2,'fsdp'=16] {'fsdp'}, use_global_device_ids=true, to_apply=%add.1 | all-reduce | flops 6912 | bytes 27648
  136.4 5.2 all-reduce
  148.2 51.1 %while.28 = (s32[]{:T(128)}, bf16[6,1,512,128]{2,3,1,0:T(8,128)(2,1)}, f32[6,1,2,512]{3,2,1,0:T(2,128)}, s32[6]{0:T(128)S(1)}, bf16[1,1024,768]{1,2,0:T(8,128)(2...) while((s32[]{:T(128)}, ...), condition=%wide.region_3.4_spmd.clone, body=%wide.region_0.3_spmd.clone.sunk | while | flops 281607168 | bytes 17078480 | solution.py:147
  202.4 16.0 %all-gather.15.cloned.1.call-done = bf16[768,3072]{1,0:T(8,128)(2,1)} async-done(((bf16[48,3072]{1,0:T(8,128)(2,1)}), bf16[768,3072]{1,0:T(8,128)(2,1)}) %all-gather.15.cloned.1.call-update) | async-done | bytes 4718608 | tf_op jit(solution)/shard_map/all_gather | solution.py:66
  218.4 20.1 %multiply_convert_fusion.1 = (bf16[512,3072]{1,0:T(8,128)(2,1)}, f32[512,3072]{1,0:T(8,128)}, f32[512,3072]{1,0:T(8,128)}) fusion(f32[3072]{0:T(1024)S(1)} %convert_element_type.264, bf16[768,3072]{1,0:T(8,128)(2,1)} %all-gather.15.cloned.1.call-done, f32[512,768]{1,0:T(8,128)S(1)} %get-tuple-element.355, f32[768]{0:T(1024)S(1)} %convert_element_type.260, ...), kind=kOutput, calls=%fused_computation.40 | convolution fusion | flops 2521694208 | bytes 22042624 | tf_op jit(solution)/shard_map/dot_general | solution.py:22
  238.5 34.4 %all-gather.17.cloned.1.call-done = bf16[3072,768]{1,0:T(8,128)(2,1)} async-done(((bf16[192,768]{1,0:T(8,128)(2,1)}), bf16[3072,768]{1,0:T(8,128)(2,1)}) %all-gather.17.cloned.1.call-update) | async-done | bytes 4718608 | tf_op jit(solution)/shard_map/all_gather | solution.py:68
  272.9 6.5 fusion.46
  283.4 10.0 %fusion.38 = (bf16[3072]{0:T(1024)(128)(2,1)}, bf16[512,3072]{1,0:T(8,128)(2,1)}) fusion(f32[512,3072]{1,0:T(8,128)} %get-tuple-element.340, f32[512,3072]{1,0:T(8,128)} %get-tuple-element.356, f32[3072]{0:T(1024)S(1)} %convert_element_type.264, bf16[512,768]{1,0:T(8,128)(2,1)S(1)} %get-tuple-element.330, bf16[3072,768]{1,0:T(8,128)(2,1)S(1)} %copy-done.38), kind=kOutput, calls=%fused_computation.115 | convolution fusion | flops 2441081856 | bytes 21252096 | tf_op jit(solution)/shard_map/dot_general | solution.py:32
  293.4 5.7 multiply_reduce_fusion.1
  305.9 109.9 %while.29 = (s32[]{:T(128)}, bf16[6,1,512,128]{2,3,1,0:T(8,128)(2,1)}, bf16[6,1,1024,128]{2,3,1,0:T(8,128)(2,1)}, bf16[6,1,1024,128]{2,3,1,0:T(8,128)(2,1)}, s32...) while((s32[]{:T(128)}, ...), condition=%wide.region_14.15_spmd.clone, body=%wide.region_12.14_spmd.clone.sunk | while | flops 687733760 | bytes 68061512 | solution.py:232
  419.3 7.0 convolution_convert_fusion.1
  427.4 6.8 convolution_convert_fusion
  435.5 5.1 reduce-scatter.12.cloned.1.call-done
  442.9 60.3 %reduce-scatter.16.cloned.1.call-done = bf16[48,768]{1,0:T(8,128)(2,1)} async-done(((bf16[768,768]{1,0:T(8,128)(2,1)}), bf16[48,768]{1,0:T(8,128)(2,1)}) %reduce-scatter.16.cloned.1.call-update) | async-done | bytes 73744 | tf_op jit(solution)/shard_map/reduce_scatter | solution.py:258
  503.2 79.0 %reduce-scatter.18.cloned.1.call-done = bf16[48,3072]{1,0:T(8,128)(2,1)} async-done(((bf16[768,3072]{1,0:T(8,128)(2,1)}), bf16[48,3072]{1,0:T(8,128)(2,1)}) %reduce-scatter.18.cloned.1.call-update) | async-done | bytes 294928 | tf_op jit(solution)/shard_map/reduce_scatter | solution.py:270
  582.2 78.3 %reduce-scatter.20.cloned.1.call-done = bf16[192,768]{1,0:T(8,128)(2,1)} async-done(((bf16[3072,768]{1,0:T(8,128)(2,1)}), bf16[192,768]{1,0:T(8,128)(2,1)}) %reduce-scatter.20.cloned.1.call-update) | async-done | bytes 294928 | tf_op jit(solution)/shard_map/reduce_scatter | solution.py:276
  660.8 27.2 %reduce-scatter.10.cloned.1.call-done = bf16[6,1,512,128]{2,3,1,0:T(8,128)(2,1)} async-done(((bf16[6,1,1024,128]{2,3,1,0:T(8,128)(2,1)}), bf16[6,1,512,128]{2,3,1,0:T(8,128)(2,1)}) %reduce-scatter.10.cloned.1.call-update) | async-done | bytes 786448 | tf_op jit(solution)/shard_map/reduce_scatter | solution.py:234
  688.1 5.4 convolution_convert_fusion.2
  696.4 61.2 %all-reduce.15 = (bf16[768]{0:T(1024)(128)(2,1)S(1)}, bf16[768]{0:T(1024)(128)(2,1)S(1)}, bf16[768]{0:T(1024)(128)(2,1)S(1)}, bf16[768]{0:T(1024)(128)(2,1)S(1)}...) all-reduce(bf16[768]{0:T(1024)(128)(2,1)S(1)} %dynamic-update-slice, ...), channel_id=1, replica_groups=mesh['ctx'=2,'fsdp'=16] {'fsdp'}, use_global_device_ids=true, to_apply=%add.7 | all-reduce | flops 8448 | bytes 33792
  759.6 6.2 add_bitcast_fusion
  784.4 67.3 %reduce-scatter.14.cloned.1.call-done = bf16[48,2304]{1,0:T(8,128)(2,1)} async-done(((bf16[768,2304]{1,0:T(8,128)(2,1)}), bf16[48,2304]{1,0:T(8,128)(2,1)}) %reduce-scatter.14.cloned.1.call-update) | async-done | bytes 221200 | tf_op jit(solution)/shard_map/reduce_scatter | solution.py:252
  851.7 6.8 all-gather.2
  (422 shorter events, 220.8 us)
Async XLA Ops:
  7.2 53.6 %all-gather.11.cloned.1.call-start = ((), (), s32[]{:S(2)}) async-start(), calls=%async_computation.7 | async-start | bytes 3760128 | tf_op jit(solution)/shard_map/all_gather | solution.py:60
  9.0 134.0 %all-gather.19.cloned.1.call-start = ((), (), s32[]{:S(2)}) async-start(), calls=%async_computation.17 | async-start | bytes 2359296 | tf_op jit(solution)/shard_map/all_gather | solution.py:114
  33.5 165.8 %copy-start.30 = (f32[768]{0:T(1024)}, f32[768]{0:T(1024)S(1)}, u32[]{:S(2)}) copy-start(f32[768]{0:T(1024)S(1)} %convert_reduce_fusion) | copy-start | bytes 9220
  65.1 69.7 %copy-start.37 = (s32[1,2]{1,0:T(1,128)S(1)}, s32[1,2]{1,0:T(1,128)}, u32[]{:S(2)}) copy-start(s32[1,2]{1,0:T(1,128)} %param.22) | copy-start | bytes 28
  65.2 69.7 %copy-start.47 = (u32[32]{0:T(128)S(1)}, u32[32]{0:T(128)}, u32[]{:S(2)}) copy-start(u32[32]{0:T(128)} %constant.143) | copy-start | bytes 388
  66.5 79.0 %all-gather.21.cloned.1.call-start = ((), (), s32[]{:S(2)}) async-start(), calls=%async_computation.18 | async-start | bytes 2359296 | tf_op jit(solution)/shard_map/all_gather | solution.py:113
  67.2 132.1 %all-gather.13.cloned.1.call-start = ((), (), s32[]{:S(2)}) async-start(), calls=%async_computation.8 | async-start | bytes 1253376 | tf_op jit(solution)/shard_map/all_gather | solution.py:62
  67.9 150.4 %all-gather.15.cloned.1.call-start = ((), (), s32[]{:S(2)}) async-start(), calls=%async_computation.9 | async-start | bytes 5013504 | tf_op jit(solution)/shard_map/all_gather | solution.py:66
  69.8 203.1 %all-gather.17.cloned.1.call-start = ((), (), s32[]{:S(2)}) async-start(), calls=%async_computation.10 | async-start | bytes 5013504 | tf_op jit(solution)/shard_map/all_gather | solution.py:68
  71.7 368.9 %reduce-scatter.12.cloned.1.call-start = ((), (), s32[]{:S(2)}) async-start(), calls=%async_computation.12 | async-start | bytes 2359296 | tf_op jit(solution)/shard_map/reduce_scatter | solution.py:237
  141.7 131.2 %copy-start.32 = (f32[768]{0:T(1024)}, f32[768]{0:T(1024)S(1)}, u32[]{:S(2)}) copy-start(f32[768]{0:T(1024)S(1)} %convert_element_type.260) | copy-start | bytes 9220
  141.7 157.5 %copy-start.20 = (f32[768]{0:T(1024)}, f32[768]{0:T(1024)S(1)}, u32[]{:S(2)}) copy-start(f32[768]{0:T(1024)S(1)} %convert_element_type.258) | copy-start | bytes 9220
  202.0 97.1 %copy-start.18 = (f32[512]{0:T(512)}, f32[512]{0:T(512)S(1)}, u32[]{:S(2)}) copy-start(f32[512]{0:T(512)S(1)} %broadcast_multiply_fusion.1) | copy-start | bytes 6148
  202.4 96.8 %copy-start.27 = (f32[512]{0:T(512)}, f32[512]{0:T(512)S(1)}, u32[]{:S(2)}) copy-start(f32[512]{0:T(512)S(1)} %fusion.30) | copy-start | bytes 6148
  415.8 87.4 %reduce-scatter.16.cloned.1.call-start = ((), (), s32[]{:S(2)}) async-start(), calls=%async_computation.14 | async-start | bytes 1253376 | tf_op jit(solution)/shard_map/reduce_scatter | solution.py:258
  419.2 163.0 %reduce-scatter.18.cloned.1.call-start = ((), (), s32[]{:S(2)}) async-start(), calls=%async_computation.15 | async-start | bytes 5013504 | tf_op jit(solution)/shard_map/reduce_scatter | solution.py:270
  426.3 234.3 %reduce-scatter.20.cloned.1.call-start = ((), (), s32[]{:S(2)}) async-start(), calls=%async_computation.16 | async-start | bytes 5013504 | tf_op jit(solution)/shard_map/reduce_scatter | solution.py:276
  434.2 253.9 %copy-start.31 = (f32[768]{0:T(1024)S(1)}, f32[768]{0:T(1024)}, u32[]{:S(2)}) copy-start(f32[768]{0:T(1024)} %copy-done.30) | copy-start | bytes 9220
  434.2 253.9 %reduce-scatter.10.cloned.1.call-start = ((), (), s32[]{:S(2)}) async-start(), calls=%async_computation.11 | async-start | bytes 2359296 | tf_op jit(solution)/shard_map/reduce_scatter | solution.py:234
  434.9 330.8 %reduce-scatter.22.cloned.1.call-start = ((), (), s32[]{:S(2)}) async-start(), calls=%async_computation.19 | async-start | bytes 208896
  442.8 336.4 %all-reduce.21.cloned.1.call-start = ((), (), s32[]{:S(2)}) async-start(), calls=%async_computation.20 | async-start | bytes 1327104 | tf_op jit(solution)/shard_map/psum | solution.py:292
  660.6 191.1 %reduce-scatter.14.cloned.1.call-start = ((), (), s32[]{:S(2)}) async-start(), calls=%async_computation.13 | async-start | bytes 3760128 | tf_op jit(solution)/shard_map/reduce_scatter | solution.py:252
  693.5 64.6 %copy-start.15 = (f32[512]{0:T(512)S(1)}, f32[512]{0:T(512)}, u32[]{:S(2)}) copy-start(f32[512]{0:T(512)} %copy-done.14) | copy-start | bytes 6148
  693.6 66.0 %copy-start.26 = (f32[512]{0:T(512)S(1)}, f32[512]{0:T(512)}, u32[]{:S(2)}) copy-start(f32[512]{0:T(512)} %copy-done.25) | copy-start | bytes 6148
  (55 other events, 330.8 us)
Sparse Core Ops, SparseCore 0:
  10.9 49.8 all-gather.10
  66.6 26.2 all-gather.18
  95.0 27.2 all-gather.20
  125.0 38.3 all-gather.12
  166.1 52.2 all-gather.14
  221.1 51.7 all-gather.16
  415.9 24.6 reduce-scatter.11
  445.2 57.9 reduce-scatter.15
  507.6 74.5 reduce-scatter.17
  585.9 74.5 reduce-scatter.19
  662.9 25.1 reduce-scatter.9
  692.0 53.6 reduce-scatter.21
  748.1 31.0 all-reduce.20
  783.5 68.1 reduce-scatter.13
